TPU v7x, 512 devices: a whole 4x4x16 slice. The times are simulated.
512 devices in a mesh: slide: 8 (over y, core), seq: 16 (over z), rep: 4 (over x).
Axes of the slice: x: 4, y: 4, z: 16, core: 2. Of those that a mesh axis runs over, the one named last changes fastest.
Arguments:
- tile_feats: bfloat16 [128, 128, 8, 1536], P(('slide', 'seq'), None, None, 'rep'), may hold values from -6 to 6
- tile_counts: int32 [8, 16, 128], P('slide'), may hold values from 0 to 8, as said below
- in_weight: bfloat16 [1536, 768], P('rep'), may hold values from -0.16871811 to 0.16871811
- norm_gain: float32 [768], replicated, may hold values from 0.1 to 1.9
- qkv_weight: bfloat16 [768, 3, 768], P(None, None, 'rep'), may hold values from -0.39687289 to 0.39687289
- out_weight: bfloat16 [768, 768], P('rep'), may hold values from -0.21875 to 0.21875
- final_gain: float32 [768], replicated, may hold values from 0.1 to 1.9
- reports: bfloat16 [1024, 768], P('rep'), may hold values from -6 to 6
- report_pair: int32 [8], P('slide'), may hold values from 0 to 1023
Outputs:
- head_out: float32 [8, 8192, 768], P('slide', 'seq', 'rep')
- slide_emb: float32 [8, 768], P('slide')
- losses: float32 [8], P('slide')
Inputs may be any that keep to these rules, and one draw needn't show every extreme that they name: tile_counts[s, j, src] is what source src sends to block j of slide s. Sources 2k and 2k + 1 together send at most 8 to one block, so that one block receives at most 512 tiles and at least 1. Some source sends exactly 8 to some block and that block receives exactly 512.
All inputs are finite; a program needn't handle non-finite values.
Results may differ from a plain program's by a relative error of at most 0.04.
Values may be sent and summed in bfloat16 or wider, within the bound.
A program may use at most 128 MiB of HBM per device.

v0:
```python
import math

import jax
import jax.numpy as jnp
from jax import lax
from jax.sharding import PartitionSpec as P

HEAD_WIDTH = 48
DILATION_STEP = 8
SLIDE_POSITIONS = 512


epsilon = 1e-05
logit_scale = 100.0


def layer_norm(value_rows, gain):
    average = jnp.mean(value_rows, axis=-1, keepdims=True)
    centred = value_rows - average
    variance = jnp.mean(centred * centred, axis=-1, keepdims=True)
    return centred / jnp.sqrt(variance + epsilon) * gain


def compact_rows(buffer, counts_col, capacity, row_total):
    sources = counts_col.shape[0]
    run_ends = jnp.cumsum(counts_col, dtype=jnp.int32)
    starts = run_ends - counts_col
    positions = jnp.arange(row_total, dtype=jnp.int32)
    passed = (run_ends[None, :] <= positions[:, None]).astype(jnp.int32)
    source = jnp.minimum(jnp.sum(passed, axis=1, dtype=jnp.int32), sources - 1)
    chosen_rows = jnp.arange(sources, dtype=jnp.int32)[None, :] == source[:, None]
    offset_in = jnp.sum(jnp.where(chosen_rows, starts[None, :], 0), axis=1, dtype=jnp.int32)
    living = positions < run_ends[sources - 1]
    slot_ids = jnp.where(living, source * capacity + positions - offset_in, 0)
    taken = jnp.take(buffer, slot_ids, axis=0)
    return (jnp.where(living[:, None], taken, jnp.zeros_like(taken)), living)


def pick_rows(value_rows, start_offset):
    reshaped_rows = value_rows.reshape(
        (value_rows.shape[0] // DILATION_STEP, DILATION_STEP) + value_rows.shape[1:]
    )
    return lax.dynamic_index_in_dim(reshaped_rows, start_offset, axis=1, keepdims=False)


def put_rows(value_rows, update, start_offset):
    reshaped_rows = value_rows.reshape(
        (value_rows.shape[0] // DILATION_STEP, DILATION_STEP) + value_rows.shape[1:]
    )
    merged = lax.dynamic_update_index_in_dim(
        reshaped_rows, jnp.expand_dims(update, 1), start_offset, 1
    )
    return merged.reshape(value_rows.shape)


def attend_block(
    queries, key_near, value_near, live_near, key_far, value_far, live_far, start_offset
):
    factor = 1.0 / math.sqrt(queries.shape[1])
    near = jnp.dot(queries, key_near.T, preferred_element_type=jnp.float32) * factor
    near = jnp.where(live_near[None, :], near, -jnp.inf)
    picked = pick_rows(queries, start_offset)
    distant = jnp.dot(picked, key_far.T, preferred_element_type=jnp.float32) * factor
    distant = jnp.where(live_far[None, :], distant, -jnp.inf)
    top_near = jnp.max(near, axis=1)
    top_far = jnp.maximum(pick_rows(top_near, start_offset), jnp.max(distant, axis=1))
    top_all = put_rows(top_near, top_far, start_offset)
    exp_near = jnp.exp(near - top_all[:, None])
    exp_far = jnp.exp(distant - top_far[:, None])
    sum_near = jnp.sum(exp_near, axis=1)
    sum_far = pick_rows(sum_near, start_offset) + jnp.sum(exp_far, axis=1)
    sum_all = put_rows(sum_near, sum_far, start_offset)
    weight_near = (exp_near / sum_all[:, None]).astype(jnp.bfloat16)
    weight_far = (exp_far / sum_far[:, None]).astype(jnp.bfloat16)
    result = jnp.dot(weight_near, value_near, preferred_element_type=jnp.float32)
    result_far = pick_rows(result, start_offset) + jnp.dot(
        weight_far, value_far, preferred_element_type=jnp.float32
    )
    result = put_rows(result, result_far, start_offset)
    return jnp.where(live_near[:, None], result, jnp.zeros_like(result))


def distant_select(arranged_rows, live_rows, start_offsets):
    row_picker = jnp.arange(DILATION_STEP, dtype=jnp.int32)[:, None] == start_offsets[None, :]
    chosen_rows = jnp.sum(
        jnp.where(row_picker[None, :, None, :, None], arranged_rows, jnp.zeros_like(arranged_rows)),
        axis=1,
    )
    live_wide = jnp.broadcast_to(live_rows[:, :, None], live_rows.shape + (start_offsets.shape[0],))
    chosen_live_mask = jnp.sum(
        jnp.where(row_picker[None], live_wide, jnp.zeros_like(live_wide)), axis=1
    )
    return (chosen_rows, chosen_live_mask)


def local(
    tile_feats,
    tile_counts,
    in_weight,
    norm_gain,
    qkv_weight,
    out_weight,
    final_gain,
    reports,
    report_pair,
):
    sources = tile_feats.shape[1]
    capacity = tile_feats.shape[2]
    feat_group = tile_feats.shape[3]
    model_width = out_weight.shape[1]
    local_heads = qkv_weight.shape[2] // HEAD_WIDTH
    counts_slide = tile_counts.reshape(tile_counts.shape[1], sources)
    block_count = counts_slide.shape[0]
    block_totals = jnp.sum(counts_slide, axis=1, dtype=jnp.int32)
    own_counts = lax.dynamic_index_in_dim(
        counts_slide, lax.axis_index("seq"), axis=0, keepdims=False
    )
    arrived = lax.all_to_all(tile_feats, ("slide", "seq"), split_axis=1, concat_axis=0, tiled=True)
    buffer = arrived.reshape(sources * capacity, feat_group)
    gathered, living = compact_rows(buffer, own_counts, capacity, SLIDE_POSITIONS)
    partial_sum = jnp.dot(gathered, in_weight, preferred_element_type=jnp.float32)
    feats = lax.psum(partial_sum.astype(jnp.bfloat16), "rep").astype(jnp.float32)
    normed = layer_norm(feats, norm_gain).astype(jnp.bfloat16)
    projected_rows = jnp.dot(
        normed,
        qkv_weight.reshape(model_width, 3 * local_heads * HEAD_WIDTH),
        preferred_element_type=jnp.float32,
    ).astype(jnp.bfloat16)
    projected_rows = projected_rows.reshape(SLIDE_POSITIONS, 3, local_heads, HEAD_WIDTH)
    start_offsets = (
        lax.axis_index("rep") * local_heads + jnp.arange(local_heads, dtype=jnp.int32)
    ) % DILATION_STEP
    lattice_rows = SLIDE_POSITIONS // DILATION_STEP
    arranged_rows = projected_rows[:, 1:3].reshape(
        lattice_rows, DILATION_STEP, 2, local_heads, HEAD_WIDTH
    )
    own_live = living.astype(jnp.bfloat16).reshape(lattice_rows, DILATION_STEP)
    chosen_rows, unused_mask = distant_select(arranged_rows, own_live, start_offsets)
    far_flat = lax.all_gather(
        chosen_rows.reshape(lattice_rows, 2 * local_heads * HEAD_WIDTH), "seq", axis=0, tiled=True
    )
    far_pairs = far_flat.reshape(far_flat.shape[0], 2, local_heads, HEAD_WIDTH)
    in_block = (
        jnp.arange(lattice_rows, dtype=jnp.int32)[:, None] * DILATION_STEP + start_offsets[None, :]
    )
    far_live = (
        (in_block[None] < block_totals[:, None, None])
        .reshape(block_count * lattice_rows, local_heads)
        .astype(jnp.float32)
    )
    results = []
    for head_index in range(local_heads):
        results.append(
            attend_block(
                projected_rows[:, 0, head_index],
                projected_rows[:, 1, head_index],
                projected_rows[:, 2, head_index],
                living,
                far_pairs[:, 0, head_index],
                far_pairs[:, 1, head_index],
                far_live[:, head_index] > 0.5,
                start_offsets[head_index],
            )
        )
    head_out = jnp.concatenate(results, axis=1)
    rep_count = lax.axis_size("rep")
    feat_sum = jnp.sum(feats, axis=0) / rep_count
    head_sum = jnp.sum(head_out, axis=0)
    pool_term = feat_sum + jnp.dot(
        head_sum, out_weight.astype(jnp.float32), precision=lax.Precision.HIGHEST
    )
    live_count = jnp.sum(living.astype(jnp.float32)) / rep_count
    pooled_sum, live_total = lax.psum((pool_term, live_count), ("seq", "rep"))
    slide_emb = layer_norm(pooled_sum / live_total, final_gain)
    unit_row = slide_emb / jnp.sqrt(jnp.sum(slide_emb * slide_emb) + 1e-06)
    report_f = reports.astype(jnp.float32)
    inverse = 1.0 / jnp.sqrt(jnp.sum(report_f * report_f, axis=1) + 1e-06)
    logits = logit_scale * jnp.dot(report_f, unit_row, precision=lax.Precision.HIGHEST) * inverse
    report_rows = reports.shape[0]
    global_ids = lax.axis_index("rep") * report_rows + jnp.arange(report_rows, dtype=jnp.int32)
    positive = jnp.sum(jnp.where(global_ids == report_pair[0], logits, 0.0))
    highest = lax.pmax(jnp.max(logits), "rep")
    mass, positive = lax.psum((jnp.sum(jnp.exp(logits - highest)), positive), "rep")
    loss_value = highest + jnp.log(mass) - positive
    return (head_out[None], slide_emb[None], loss_value.reshape(1))


def solution(mesh):
    in_specs = (
        P(("slide", "seq"), None, None, "rep"),
        P("slide", None, None),
        P("rep", None),
        P(),
        P(None, None, "rep"),
        P("rep", None),
        P(),
        P("rep", None),
        P("slide"),
    )
    out_specs = (P("slide", "seq", "rep"), P("slide", None), P("slide"))
    return jax.shard_map(local, mesh=mesh, in_specs=in_specs, out_specs=out_specs, check_vma=False)
```

profile of v0, /device:TPU:24, one launch (start us, length us, event | category | flops | bytes accessed | tf_op | source)
XLA Modules:
  0.0 417.6 jit_solution(9728713551326497108)
XLA Ops:
  7.2 20.0 %all-to-all-start = ((bf16[1,128,8,384]{3,2,0,1:T(8,128)(2,1)}), bf16[1,128,8,384]{3,2,0,1:T(8,128)(2,1)S(1)}, u32[]{:S(2)}, u32[]{:S(2)}) async-start(bf16[1,128,8,384]{3,2,0,1:T(8,128)(2,1)} %bitcast.194), calls=%async_computation | async-start | bytes 1572864 | tf_op jit(solution)/shard_map/all_to_all | solution.py:118
  30.1 37.4 %all-to-all-done = bf16[1,128,8,384]{3,2,0,1:T(8,128)(2,1)S(1)} async-done(((bf16[1,128,8,384]{3,2,0,1:T(8,128)(2,1)}), bf16[1,128,8,384]{3,2,0,1:T(8,128)(2,1)S(1)}, u32[]{:S(2)}, u32[]{:S(2)}) %all-to-all-start) | async-done | bytes 786464 | tf_op jit(solution)/shard_map/all_to_all | solution.py:118
  67.6 1.9 gather_fusion
  69.5 1.5 convolution_convert_fusion
  76.8 1.3 convert_reduce_fusion.3
  82.8 0.7 multiply_reduce_fusion
  83.6 42.5 %all-reduce.4.cloned.1.call-done = bf16[512,768]{1,0:T(8,128)(2,1)} async-done(((bf16[512,768]{1,0:T(8,128)(2,1)}), bf16[512,768]{1,0:T(8,128)(2,1)}) %all-reduce.4.cloned.1.call-update) | async-done | bytes 786448 | tf_op jit(solution)/shard_map/psum | solution.py:122
  126.2 1.4 convert_reduce_fusion.1
  127.6 0.9 convert_reduce_fusion
  128.5 0.8 convolution_convert_fusion.1
  129.4 0.7 fusion.69
  130.2 1.3 fusion.77
  131.5 1.9 fusion.75
  133.4 1.9 fusion.73
  135.3 1.9 fusion.71
  137.7 0.8 fusion.13
  138.7 34.9 %all_gather.3 = bf16[1024,384]{1,0:T(8,128)(2,1)S(1)} all-gather(bf16[64,384]{1,0:T(8,128)(2,1)S(1)} %reshape.313), channel_id=1, replica_groups=mesh['slide'=8,'seq'=16,'rep'=4] {'seq'}, dimensions={0}, use_global_device_ids=true | all-gather | bytes 835584 | tf_op jit(solution)/shard_map/all_gather | solution.py:139
  176.5 1.2 fusion.24
  178.3 1.8 dynamic_update_slice.46
  180.2 1.1 copy.126
  181.2 0.9 copy.115
  182.9 1.0 fusion.76
  184.6 0.8 reshape.317
  185.4 1.6 fusion.64
  187.4 0.7 fusion.35
  188.2 1.3 copy.118
  189.5 0.9 dynamic_update_slice.41
  191.1 1.5 fusion.15
  192.7 0.8 reshape.318
  193.4 2.1 fusion.63
  195.5 1.1 dynamic_update_slice.42
  197.3 1.2 fusion.26
  199.2 1.8 dynamic_update_slice.43
  201.1 1.7 copy.120
  202.8 0.9 copy.127
  204.4 1.0 fusion.74
  206.2 0.8 reshape.323
  206.9 1.6 fusion.68
  209.8 1.3 copy.130
  211.1 0.9 dynamic_update_slice.47
  212.7 1.5 fusion.17
  214.3 0.8 reshape.324
  215.0 2.1 fusion.67
  217.1 0.9 dynamic_update_slice.48
  218.7 1.2 fusion.22
  220.6 1.8 dynamic_update_slice.49
  222.5 1.7 copy.132
  224.4 1.0 fusion.72
  225.5 0.8 reshape.311
  226.3 0.8 fusion.62
  227.4 0.9 dynamic_update_slice.38
  228.8 0.8 fusion.61
  229.6 0.9 dynamic_update_slice.39
  230.5 1.2 fusion.28
  232.4 1.8 dynamic_update_slice.40
  234.2 1.1 copy.114
  235.4 0.8 fusion.38
  236.4 143.6 %all-reduce = (f32[768]{0:T(1024)S(1)}, f32[]{:T(128)}) all-reduce(f32[768]{0:T(1024)S(1)} %multiply_add_fusion, f32[]{:T(128)S(6)} %div.161), channel_id=1, replica_groups=mesh['slide'=8,'seq'=16,'rep'=4] {'seq','rep'}, use_global_device_ids=true, to_apply=%region_26.27 | all-reduce | flops 769 | bytes 6152 | tf_op jit(solution)/shard_map/psum | solution.py:173
  380.1 1.2 fusion.55
  382.0 1.3 multiply_reduce_fusion.2
  383.9 1.3 multiply_reduce_fusion.1
  387.5 8.3 %pmax.7 = f32[]{:T(128)} all-reduce(f32[]{:T(128)} %fusion.56), channel_id=1, replica_groups=mesh['slide'=8,'seq'=16,'rep'=4] {'rep'}, use_global_device_ids=true, to_apply=%region_34.35 | all-reduce | flops 1 | bytes 8 | tf_op jit(solution)/shard_map/pmax | solution.py:182
  395.9 1.3 fusion.50
  397.2 10.4 %all-reduce.1 = (f32[]{:T(128)}, f32[]{:T(128)}) all-reduce(f32[]{:T(128)} %get-tuple-element.10, f32[]{:T(128)} %get-tuple-element.9), channel_id=1, replica_groups=mesh['slide'=8,'seq'=16,'rep'=4] {'rep'}, use_global_device_ids=true, to_apply=%region_36.37 | all-reduce | flops 2 | bytes 16 | tf_op jit(solution)/shard_map/psum | solution.py:183
  (144 shorter events, 21.3 us)
Async XLA Ops:
  7.2 121.4 %copy-start = (bf16[768,3,192]{0,2,1:T(8,128)(2,1)S(1)}, bf16[768,3,192]{0,2,1:T(8,128)(2,1)}, u32[]{:S(2)}) copy-start(bf16[768,3,192]{0,2,1:T(8,128)(2,1)} %param.13) | copy-start | bytes 2654212
  7.2 20.0 %copy-start.16 = (s32[1,16,128]{2,1,0:T(8,128)S(1)}, s32[1,16,128]{2,1,0:T(8,128)}, u32[]{:S(2)}) copy-start(s32[1,16,128]{2,1,0:T(8,128)} %param.10) | copy-start | bytes 24580
  7.2 60.4 %all-to-all-start = ((bf16[1,128,8,384]{3,2,0,1:T(8,128)(2,1)}), bf16[1,128,8,384]{3,2,0,1:T(8,128)(2,1)S(1)}, u32[]{:S(2)}, u32[]{:S(2)}) async-start(bf16[1,128,8,384]{3,2,0,1:T(8,128)(2,1)} %bitcast.194), calls=%async_computation | async-start | bytes 1572864 | tf_op jit(solution)/shard_map/all_to_all | solution.py:118
  27.2 99.0 %all-reduce.4.cloned.1.call-start = ((), (), s32[]{:S(2)}) async-start(), calls=%async_computation.1 | async-start | bytes 1572864 | tf_op jit(solution)/shard_map/psum | solution.py:122
  30.1 105.2 %copy-start.23 = (pred[512]{0:T(512)(128)(4,1)}, pred[512]{0:T(512)(128)(4,1)S(1)}, u32[]{:S(2)}) copy-start(pred[512]{0:T(512)(128)(4,1)S(1)} %get-tuple-element.65) | copy-start | bytes 1540
  67.6 1.9 copy-start.27
  71.1 11.8 %copy-start.2 = (bf16[256,768]{1,0:T(8,128)(2,1)S(1)}, bf16[256,768]{1,0:T(8,128)(2,1)}, u32[]{:S(2)}) copy-start(bf16[256,768]{1,0:T(8,128)(2,1)} %param.16) | copy-start | bytes 1179652
  78.2 50.4 %copy-start.28 = (f32[768]{0:T(1024)S(1)}, f32[768]{0:T(1024)}, u32[]{:S(2)}) copy-start(f32[768]{0:T(1024)} %param.12) | copy-start | bytes 9220
  126.2 1.4 copy-start.1
  129.4 5.9 %copy-start.7 = (bf16[512,576]{0,1:T(8,128)(2,1)}, bf16[512,576]{0,1:T(8,128)(2,1)S(1)}, u32[]{:S(2)}) copy-start(bf16[512,576]{0,1:T(8,128)(2,1)S(1)} %convolution_convert_fusion.1) | copy-start | bytes 1769476
  173.9 1.6 copy-start.6
  177.6 0.7 copy-start.11
  178.3 12.8 %copy-start.5 = (f32[512,512]{1,0:T(8,128)S(1)}, f32[512,512]{1,0:T(8,128)}, u32[]{:S(2)}) copy-start(f32[512,512]{1,0:T(8,128)} %get-tuple-element.58) | copy-start | bytes 3145732
  187.0 0.5 copy-start.19
  197.3 1.3 copy-start.20
  197.3 1.3 copy-start.25
  198.5 0.7 copy-start.12
  199.2 13.5 %copy-start.4 = (f32[512,512]{1,0:T(8,128)S(1)}, f32[512,512]{1,0:T(8,128)}, u32[]{:S(2)}) copy-start(f32[512,512]{1,0:T(8,128)} %get-tuple-element.54) | copy-start | bytes 3145732
  208.5 0.6 copy-start.21
  218.7 1.3 copy-start.22
  218.7 1.3 copy-start.26
  219.9 0.7 copy-start.13
  220.6 7.7 %copy-start.3 = (f32[512,512]{1,0:T(8,128)S(1)}, f32[512,512]{1,0:T(8,128)}, u32[]{:S(2)}) copy-start(f32[512,512]{1,0:T(8,128)} %get-tuple-element.50) | copy-start | bytes 3145732
  231.7 0.7 copy-start.10
  231.7 3.6 copy-start.8
  231.8 3.6 copy-start.9
  231.8 3.6 copy-start.24
  232.4 3.7 copy-start.14
  234.2 2.2 copy-start.15
  235.3 148.6 %copy-start.18 = (f32[768]{0:T(1024)S(1)}, f32[768]{0:T(1024)}, u32[]{:S(2)}) copy-start(f32[768]{0:T(1024)} %param.15) | copy-start | bytes 9220
  235.3 150.9 %copy-start.17 = (f32[256]{0:T(256)S(1)}, f32[256]{0:T(256)}, u32[]{:S(2)}) copy-start(f32[256]{0:T(256)} %multiply_reduce_fusion) | copy-start | bytes 3076
Sparse Core Ops, SparseCore 0:
  71.2 54.9 all-reduce.3
where the time goes:
time: 420 us; the launch traced here: 418 us
  blocking collectives  197 us (47%)
  waiting for transfers between devices  80 us (19%)
  local copies, waits for them, and re-layouts  43 us (10%)
  other arithmetic  29.4 us (7%)
  between operations  28.8 us (7%)
  starting transfers between devices  20 us (5%)
  matrix products  19.1 us (5%)
    psum x1, blocking collectives, local(): pooled_sum, live_total = lax.psum((pool_term, live_count), ('seq', 'rep'))  144 us
    psum x1, waiting for transfers between devices, local(): lax.psum(partial_sum.astype(jnp.bfloat16), 'rep').astype(jnp.float32)  42.5 us
    all_to_all x1, waiting for transfers between devices, local(): lax.all_to_all(tile_feats, ('slide', 'seq'), split_axis=1, concat_axis=0,...  37.4 us
    all_gather x1, blocking collectives, local(): lax.all_gather(chosen_rows.reshape(lattice_rows, 2 * local_heads * HEAD_W...  34.9 us
    all_to_all x1, starting transfers between devices, local(): lax.all_to_all(tile_feats, ('slide', 'seq'), split_axis=1, concat_axis=0,...  20 us
    dynamic_update_slice x12, local copies, waits for them, and re-layouts, put_rows(): lax.dynamic_update_index_in_dim(reshaped_rows, jnp.expand_dims(update, 1)...  13.4 us
    psum x1, blocking collectives, local(): lax.psum((jnp.sum(jnp.exp(logits - highest)), positive), 'rep')  10.4 us
  transfers between devices with their start and end apart: 2, of which 2 were waited for; matrix products, arithmetic and copies ran while one was open for 2% of the time, Pallas kernels for 0%

commit v1 on v0

v1 whole, which is shorter than its diff:
```python
import functools
import math

import jax
import jax.numpy as jnp
from jax import lax
from jax.experimental import pallas as pl
from jax.experimental.pallas import tpu as pltpu
from jax.sharding import PartitionSpec as P

HEAD_WIDTH = 48
STEP = 8
EPS = 1e-05
LOGIT_SCALE = 100.0
NEG = -1e30
MESH = pl.DeviceIdType.MESH
F32 = jnp.float32
BF16 = jnp.bfloat16


def to_peer(src, dst, send, recv, axis, peer):
    return pltpu.make_async_remote_copy(
        src_ref=src, dst_ref=dst, send_sem=send, recv_sem=recv,
        device_id={axis: peer}, device_id_type=MESH,
    )


def share(buf, send, recv, axis, me, n):
    def one(d, _):
        to_peer(buf.at[me], buf.at[me], send.at[d], recv.at[me], axis, lax.rem(me + d, n)).start()
        return 0

    lax.fori_loop(1, n, one, 0)


def shared(buf, send, recv, axis, me, n):
    def one(d, _):
        slot = lax.rem(me + d, n)
        to_peer(buf.at[me], buf.at[slot], send.at[d], recv.at[slot], axis, slot).wait()
        return 0

    lax.fori_loop(1, n, one, 0)


def encoder_kernel(
    n_seq, n_rep,
    feats_ref, counts_ref, gain_ref, wqkv_ref, wout_ref, fgain_ref, reports_ref, pair_ref,
    out_ref, emb_ref, loss_ref,
    normed, q_s, k_s, v_s, kv_all, m_s, l_s, outn, natural, fbuf, hbuf, rbuf, sbuf,
    kv_recv, right_send, left_send, f_send, f_recv, h_send, h_recv, r_send, r_recv, s_send, s_recv,
):
    seq = lax.axis_index("seq")
    rep = lax.axis_index("rep")
    rows, width = normed.shape
    heads = m_s.shape[0]
    part = heads * HEAD_WIDTH
    lattice = rows // STEP
    wide = q_s.shape[1]
    scale = math.log2(math.e) / math.sqrt(HEAD_WIDTH)
    chunk = 128
    half = lax.rem(rep * heads, STEP) * lattice
    far_rows = heads * lattice

    barrier = pltpu.get_barrier_semaphore()

    def greet(axis, me, n):
        def one(d, _):
            pl.semaphore_signal(barrier, inc=1, device_id={axis: lax.rem(me + d, n)}, device_id_type=MESH)
            return 0

        lax.fori_loop(1, n, one, 0)

    greet("seq", seq, n_seq)
    greet("rep", rep, n_rep)

    counts = counts_ref[...].astype(F32)
    blocks = lax.broadcasted_iota(jnp.int32, counts.shape, 0)
    own_total = jnp.sum(jnp.where(blocks == seq, counts, 0.0), keepdims=True)
    slide_total = jnp.sum(counts, keepdims=True)

    def norm_rows(start):
        values = feats_ref[pl.ds(start, chunk), :].astype(F32)
        centred = values - jnp.mean(values, axis=1, keepdims=True)
        variance = jnp.mean(centred * centred, axis=1, keepdims=True)
        normed[pl.ds(start, chunk), :] = (centred * lax.rsqrt(variance + EPS) * gain_ref[...]).astype(BF16)
        return jnp.sum(values, axis=0, keepdims=True)

    feat_sum = jnp.zeros((1, width), F32)
    for index in range(far_rows // chunk):
        feat_sum += norm_rows(pl.multiple_of(half + index * chunk, chunk))

    far_kv = jnp.dot(
        normed[pl.ds(pl.multiple_of(half, far_rows), far_rows), :], wqkv_ref[:, wide:],
        preferred_element_type=F32,
    )
    lane = lax.broadcasted_iota(jnp.int32, (1, wide), 1)
    far_k = jnp.zeros((lattice, wide), F32)
    far_v = jnp.zeros((lattice, wide), F32)
    for head in range(heads):
        own = (lane >= head * HEAD_WIDTH) & (lane < (head + 1) * HEAD_WIDTH)
        block = far_kv[head * lattice:(head + 1) * lattice]
        far_k = jnp.where(own, block[:, :wide], far_k)
        far_v = jnp.where(own, block[:, wide:], far_v)
    low = lax.broadcasted_iota(jnp.int32, (1, 128), 1) < 64
    mixed = jnp.where(low, far_k[:, 128:], pltpu.roll(far_v[:, 128:], 64, 1))
    kv_all[seq] = jnp.concatenate([far_k[:, :128], mixed, far_v[:, :128]], axis=1).astype(BF16)

    pl.semaphore_wait(barrier, n_seq + n_rep - 2)
    right, left = lax.rem(seq + 1, n_seq), lax.rem(seq + n_seq - 1, n_seq)
    rights, lefts = n_seq // 2, n_seq - 1 - n_seq // 2

    def go_right(step):
        slot = lax.rem(seq - step + n_seq, n_seq)
        return to_peer(kv_all.at[slot], kv_all.at[slot], right_send.at[step], kv_recv.at[slot], "seq", right)

    def go_left(step):
        slot = lax.rem(seq + step, n_seq)
        return to_peer(kv_all.at[slot], kv_all.at[slot], left_send.at[step], kv_recv.at[slot], "seq", left)

    def arrived(slot):
        to_peer(kv_all.at[slot], kv_all.at[slot], right_send.at[0], kv_recv.at[slot], "seq", right).wait_recv()

    go_right(0).start()
    go_left(0).start()

    other = lax.rem(half + far_rows, rows)
    for index in range((rows - far_rows) // chunk):
        feat_sum += norm_rows(pl.multiple_of(other + index * chunk, chunk))
    fbuf[seq] = feat_sum
    share(fbuf, f_send, f_recv, "seq", seq, n_seq)

    row_id = lax.broadcasted_iota(jnp.int32, (rows, 1), 0)
    position = lax.rem(row_id, lattice) * STEP + lax.div(row_id, lattice)
    live_rows = position.astype(F32) < own_total

    def project(index, _):
        at = pl.ds(pl.multiple_of(index * chunk, chunk), chunk)
        three = jnp.dot(normed[at, :], wqkv_ref[...], preferred_element_type=F32)
        ids = lax.broadcasted_iota(jnp.int32, (chunk, 1), 0) + index * chunk
        place = lax.rem(ids, lattice) * STEP + lax.div(ids, lattice)
        bias = jnp.where(place.astype(F32) < own_total, 0.0, NEG)
        q_s[at, :] = jnp.where(lane == part, 1.0, three[:, :wide]).astype(BF16)
        k_s[at, :] = jnp.where(lane == part, bias, three[:, wide:2 * wide]).astype(BF16)
        v_s[at, :] = jnp.where(lane == part, 1.0, three[:, 2 * wide:]).astype(BF16)
        return 0

    lax.fori_loop(0, rows // chunk, project, 0)
    outn[...] = jnp.zeros_like(outn)

    def near(piece):
        head = lax.div(piece, rows // chunk)
        at = pl.ds(pl.multiple_of(lax.rem(piece, rows // chunk) * chunk, chunk), chunk)
        own = (lane >= head * HEAD_WIDTH) & (lane < (head + 1) * HEAD_WIDTH)
        queries = q_s[at, :]
        queries = jnp.where(own | (lane == part), queries, jnp.zeros_like(queries))
        scores = lax.dot_general(queries, k_s[...], (((1,), (1,)), ((), ())), preferred_element_type=F32)
        top = jnp.max(scores, axis=1, keepdims=True)
        weights = jnp.exp2((scores - top) * scale).astype(BF16)
        result = jnp.dot(weights, v_s[...], preferred_element_type=F32)
        mass = jnp.sum(jnp.where(lane == part, result, 0.0), axis=1, keepdims=True)
        m_s[head, at, :] = top
        l_s[head, at, :] = mass
        outn[at, :] = jnp.where(own, result * (1.0 / mass), outn[at, :])

    pieces = heads * (rows // chunk)
    per_step = pieces // rights

    def ring(step, _):
        @pl.when(step >= 1)
        def _():
            arrived(lax.rem(seq - step + n_seq, n_seq))
            go_right(step).start()

            @pl.when(step <= lefts)
            def _():
                arrived(lax.rem(seq + step, n_seq))

            @pl.when(step < lefts)
            def _():
                go_left(step).start()

        for index in range(per_step):
            near(step * per_step + index)
        return 0

    lax.fori_loop(0, rights, ring, 0)

    keys = n_seq * lattice
    key_block = lax.broadcasted_iota(jnp.int32, (n_seq, keys), 1) // lattice
    block_id = lax.broadcasted_iota(jnp.int32, (n_seq, keys), 0)
    spread = jnp.where(key_block == block_id, 1.0, 0.0).astype(BF16)
    wide_counts = lax.dot_general(counts.astype(BF16), spread, (((0,), (0,)), ((), ())), preferred_element_type=F32)
    key_total = jnp.dot(jnp.ones((8, counts.shape[1]), BF16), wide_counts.astype(BF16), preferred_element_type=F32)[:1]
    key_place = (lax.rem(lax.broadcasted_iota(jnp.int32, (1, keys), 1), lattice) * STEP).astype(F32)
    report_rows = reports_ref[...].astype(F32)
    inverse = LOGIT_SCALE * lax.rsqrt(jnp.sum(report_rows * report_rows, axis=1, keepdims=True) + 1e-06)

    arrived(lax.rem(seq - rights + n_seq, n_seq))

    keys_far = kv_all[...].reshape(keys, 3 * 128)
    for head in range(heads):
        own = (lane >= head * HEAD_WIDTH) & (lane < (head + 1) * HEAD_WIDTH)
        start = pl.multiple_of(half + head * lattice, lattice)
        at = pl.ds(start, lattice)
        queries = q_s[at, :]
        queries = jnp.where(own, queries, jnp.zeros_like(queries))
        scores = lax.dot_general(queries, keys_far[:, :wide], (((1,), (1,)), ((), ())), preferred_element_type=F32)
        offset = lax.div(start, lattice).astype(F32)
        scores = jnp.where(key_place + offset < key_total, scores, NEG)
        top_far = jnp.max(scores, axis=1, keepdims=True)
        weights = jnp.exp2((scores - top_far) * scale)
        mass_far = jnp.sum(weights, axis=1, keepdims=True)
        mixed = jnp.dot(weights.astype(BF16), keys_far[:, 128:], preferred_element_type=F32)
        result = jnp.concatenate([mixed[:, 128:], pltpu.roll(mixed[:, :128], 64, 1)], axis=1)
        top_near = m_s[head, at, :]
        top = jnp.maximum(top_near, top_far)
        keep_near = l_s[head, at, :] * jnp.exp2((top_near - top) * scale)
        keep_far = jnp.exp2((top_far - top) * scale)
        inverse_mass = 1.0 / (keep_near + mass_far * keep_far)
        before = outn[at, :]
        merged = before * (keep_near * inverse_mass) + result * (keep_far * inverse_mass)
        outn[at, :] = jnp.where(own, merged, before)

    final = jnp.where(live_rows, outn[...], 0.0)
    hbuf[seq] = jnp.sum(final, axis=0, keepdims=True)
    share(hbuf, h_send, h_recv, "seq", seq, n_seq)
    for offset in range(STEP):
        for tile in range(wide // 128):
            natural[tile, pl.ds(offset, lattice, stride=STEP), :] = final[
                offset * lattice:(offset + 1) * lattice, tile * 128:(tile + 1) * 128
            ]
    for tile in range(wide // 128):
        end = min(part, (tile + 1) * 128)
        out_ref[:, tile * 128:end] = natural[tile, :, :end - tile * 128]
    shared(fbuf, f_send, f_recv, "seq", seq, n_seq)
    feat_total = jnp.sum(fbuf[...], axis=0)
    shared(hbuf, h_send, h_recv, "seq", seq, n_seq)
    head_total = jnp.sum(hbuf[...], axis=0)
    high = head_total.astype(BF16)
    rest = head_total - high.astype(F32)
    middle = rest.astype(BF16)
    lowest = (rest - middle.astype(F32)).astype(BF16)
    row8 = lax.broadcasted_iota(jnp.int32, (8, wide), 0)
    stacked = jnp.where(row8 == 0, high.astype(F32), 0.0)
    stacked = jnp.where(row8 == 1, middle.astype(F32), stacked)
    stacked = jnp.where(row8 == 2, lowest.astype(F32), stacked).astype(BF16)
    term = jnp.sum(jnp.dot(stacked[:, :part], wout_ref[...], preferred_element_type=F32), axis=0, keepdims=True)
    rbuf[rep] = term
    share(rbuf, r_send, r_recv, "rep", rep, n_rep)
    shared(rbuf, r_send, r_recv, "rep", rep, n_rep)
    pooled = (feat_total + jnp.sum(rbuf[...], axis=0)) / slide_total
    centred = pooled - jnp.mean(pooled, axis=1, keepdims=True)
    variance = jnp.mean(centred * centred, axis=1, keepdims=True)
    emb = centred / jnp.sqrt(variance + EPS) * fgain_ref[...]
    emb_ref[...] = emb
    unit = emb / jnp.sqrt(jnp.sum(emb * emb, axis=1, keepdims=True) + 1e-06)
    logits = jnp.sum(report_rows * unit, axis=1, keepdims=True) * inverse
    ids = lax.broadcasted_iota(jnp.int32, logits.shape, 0) + rep * logits.shape[0]
    positive = jnp.sum(jnp.where(ids == pair_ref[0], logits, 0.0), keepdims=True)
    top = jnp.max(logits, keepdims=True)
    mass = jnp.sum(jnp.exp(logits - top), keepdims=True)
    lane1 = lax.broadcasted_iota(jnp.int32, (1, 128), 1)
    sbuf[rep] = jnp.where(lane1 == 0, top, jnp.where(lane1 == 1, mass, jnp.where(lane1 == 2, positive, 0.0)))
    share(sbuf, s_send, s_recv, "rep", rep, n_rep)
    shared(sbuf, s_send, s_recv, "rep", rep, n_rep)
    every = sbuf[...]
    tops, masses, positives = every[:, :, 0:1], every[:, :, 1:2], every[:, :, 2:3]
    highest = jnp.max(tops, axis=0)
    total = jnp.sum(masses * jnp.exp(tops - highest[None]), axis=0)
    loss_ref[...] = highest + jnp.log(total) - jnp.sum(positives, axis=0)

    def sent_right(step, _):
        go_right(step).wait_send()
        return 0

    def sent_left(step, _):
        go_left(step).wait_send()
        return 0

    lax.fori_loop(0, rights, sent_right, 0)
    lax.fori_loop(0, lefts, sent_left, 0)


def encoder(n_seq, n_rep, feats, counts, gain, wqkv, wout, fgain, reports, pair):
    rows, width = feats.shape
    part = wout.shape[0]
    heads = part // HEAD_WIDTH
    wide = wqkv.shape[1] // 3
    lattice = rows // STEP
    dma = pltpu.SemaphoreType.DMA
    vmem = pl.BlockSpec(memory_space=pltpu.VMEM)
    return pl.pallas_call(
        functools.partial(encoder_kernel, n_seq, n_rep),
        out_shape=(
            jax.ShapeDtypeStruct((rows, part), F32),
            jax.ShapeDtypeStruct((1, width), F32),
            jax.ShapeDtypeStruct((1, 1), F32),
        ),
        in_specs=[vmem] * 7 + [pl.BlockSpec(memory_space=pltpu.SMEM)],
        out_specs=(vmem, vmem, vmem),
        scratch_shapes=[
            pltpu.VMEM((rows, width), BF16),
            pltpu.VMEM((rows, wide), BF16),
            pltpu.VMEM((rows, wide), BF16),
            pltpu.VMEM((rows, wide), BF16),
            pltpu.VMEM((n_seq, lattice, 3 * 128), BF16),
            pltpu.VMEM((heads, rows, 1), F32),
            pltpu.VMEM((heads, rows, 1), F32),
            pltpu.VMEM((rows, wide), F32),
            pltpu.VMEM((wide // 128, rows, 128), F32),
            pltpu.VMEM((n_seq, 1, width), F32),
            pltpu.VMEM((n_seq, 1, wide), F32),
            pltpu.VMEM((n_rep, 1, width), F32),
            pltpu.VMEM((n_rep, 1, 128), F32),
            dma((n_seq,)),
            dma((n_seq,)),
            dma((n_seq,)),
            dma((n_seq,)),
            dma((n_seq,)),
            dma((n_seq,)),
            dma((n_seq,)),
            dma((n_rep,)),
            dma((n_rep,)),
            dma((n_rep,)),
            dma((n_rep,)),
        ],
        compiler_params=pltpu.CompilerParams(
            collective_id=0, has_side_effects=True, vmem_limit_bytes=48 * 1024 * 1024
        ),
    )(feats, counts, gain, wqkv, wout, fgain, reports, pair)


def compact_rows(buffer, counts_col, capacity, row_total):
    sources = counts_col.shape[0]
    run_ends = jnp.cumsum(counts_col, dtype=jnp.int32)
    starts = run_ends - counts_col
    order = jnp.arange(row_total, dtype=jnp.int32)
    lattice = row_total // STEP
    positions = (order % lattice) * STEP + order // lattice
    passed = (run_ends[None, :] <= positions[:, None]).astype(jnp.int32)
    source = jnp.minimum(jnp.sum(passed, axis=1, dtype=jnp.int32), sources - 1)
    chosen_rows = jnp.arange(sources, dtype=jnp.int32)[None, :] == source[:, None]
    offset_in = jnp.sum(jnp.where(chosen_rows, starts[None, :], 0), axis=1, dtype=jnp.int32)
    living = positions < run_ends[sources - 1]
    slot_ids = jnp.where(living, source * capacity + positions - offset_in, 0)
    taken = jnp.take(buffer, slot_ids, axis=0)
    return jnp.where(living[:, None], taken, jnp.zeros_like(taken))


def local(tile_feats, tile_counts, in_weight, norm_gain, qkv_weight, out_weight, final_gain, reports, report_pair):
    sources, capacity, feat_group = tile_feats.shape[1:]
    rows = 512
    width = out_weight.shape[1]
    part = qkv_weight.shape[2]
    wide = -(-part // 128) * 128
    counts = tile_counts.reshape(tile_counts.shape[1], sources)
    own_counts = lax.dynamic_index_in_dim(counts, lax.axis_index("seq"), axis=0, keepdims=False)
    arrived = lax.all_to_all(tile_feats, ("slide", "seq"), split_axis=1, concat_axis=0, tiled=True)
    gathered = compact_rows(arrived.reshape(sources * capacity, feat_group), own_counts, capacity, rows)
    partial_sum = jnp.dot(gathered, in_weight, preferred_element_type=F32)
    feats = lax.psum(partial_sum.astype(BF16), "rep")
    wqkv = jnp.pad(qkv_weight, ((0, 0), (0, 0), (0, wide - part))).reshape(width, 3 * wide)
    head_out, emb, loss = encoder(
        lax.axis_size("seq"), lax.axis_size("rep"), feats, counts, norm_gain.reshape(1, width), wqkv,
        out_weight, final_gain.reshape(1, width), reports, report_pair,
    )
    return head_out[None], emb, loss.reshape(1)


def solution(mesh):
    in_specs = (
        P(("slide", "seq"), None, None, "rep"),
        P("slide", None, None),
        P("rep", None),
        P(),
        P(None, None, "rep"),
        P("rep", None),
        P(),
        P("rep", None),
        P("slide"),
    )
    out_specs = (P("slide", "seq", "rep"), P("slide", None), P("slide"))
    return jax.shard_map(local, mesh=mesh, in_specs=in_specs, out_specs=out_specs, check_vma=False)
```

time: 420 us -> 195 us (0.46)
  blocking collectives: 197 us -> 0 us
  Pallas kernels: 0 us -> 57.4 us
  local copies, waits for them, and re-layouts: 43 us -> 7.99 us
  other arithmetic: 29.4 us -> 2.09 us
  matrix products: 19.1 us -> 1.52 us
  between operations: 28.8 us -> 16.6 us
  waiting for transfers between devices: 80 us -> 89.1 us
    psum x2 -> x0, blocking collectives: 154 us -> none  [the longest x1 144 us: local(): pooled_sum, live_total = lax.psum((pool_term, live_count), ('seq', 'rep'))]
    pallas_call x0 -> x1, Pallas kernels: none -> 57.4 us  [encoder(): pl.pallas_call(functools.partial(encoder_kernel, n_seq, n_rep), out_shape...]
    all_gather x1 -> x0, blocking collectives: 34.9 us -> none  [local(): lax.all_gather(chosen_rows.reshape(lattice_rows, 2 * local_heads * HEAD_W...]
    dot_general x20 -> x1, matrix products: 19.1 us -> 1.52 us  [local(): partial_sum = jnp.dot(gathered, in_weight, preferred_element_type=F32)]
    reduce_sum x19 -> x0, other arithmetic: 16.6 us -> none  [the longest x4 3.65 us: attend_block(): sum_near = jnp.sum(exp_near, axis=1)]
    dynamic_update_slice x12 -> x0, local copies, waits for them, and re-layouts: 13.4 us -> none  [put_rows(): lax.dynamic_update_index_in_dim(reshaped_rows, jnp.expand_dims(update, 1)...]
    psum x1, waiting for transfers between devices: 42.5 us -> 51.6 us  [local(): feats = lax.psum(partial_sum.astype(BF16), 'rep')]
    pmax x1 -> x0, blocking collectives: 8.35 us -> none  [local(): highest = lax.pmax(jnp.max(logits), 'rep')]
  transfers between devices with their start and end apart: 2 -> 2, of which waited for: 2 -> 2; matrix products, arithmetic and copies ran while one was open for 2% -> 3% of each run, Pallas kernels for 0% -> 0%
where the time goes in v1:
time: 195 us
  waiting for transfers between devices  89.1 us (46%)
  Pallas kernels  57.4 us (29%)
  starting transfers between devices  20 us (10%)
  between operations  16.6 us (9%)
  local copies, waits for them, and re-layouts  7.99 us (4%)
  other arithmetic  2.09 us (1%)
    pallas_call x1, Pallas kernels, encoder(): pl.pallas_call(functools.partial(encoder_kernel, n_seq, n_rep), out_shape...  57.4 us
    psum x1, waiting for transfers between devices, local(): feats = lax.psum(partial_sum.astype(BF16), 'rep')  51.6 us
    all_to_all x1, waiting for transfers between devices, local(): lax.all_to_all(tile_feats, ('slide', 'seq'), split_axis=1, concat_axis=0,...  37.6 us
    all_to_all x1, starting transfers between devices, local(): lax.all_to_all(tile_feats, ('slide', 'seq'), split_axis=1, concat_axis=0,...  20 us
  transfers between devices with their start and end apart: 2, of which 2 were waited for; matrix products, arithmetic and copies ran while one was open for 3% of the time, Pallas kernels for 0%

profile of v1, /device:TPU:24, one launch (start us, length us, event | category | flops | bytes accessed | tf_op | source)
XLA Modules:
  0.0 194.7 jit_solution(1193437110065708027)
XLA Ops:
  7.2 0.0 copy-start
  7.2 0.0 copy-start.4
  7.2 20.0 %all-to-all-start = ((bf16[1,128,8,384]{3,2,0,1:T(8,128)(2,1)}), bf16[1,128,8,384]{3,2,0,1:T(8,128)(2,1)S(1)}, u32[]{:S(2)}, u32[]{:S(2)}) async-start(bf16[1,128,8,384]{3,2,0,1:T(8,128)(2,1)} %bitcast.19), calls=%async_computation | async-start | bytes 1572864 | tf_op jit(solution)/shard_map/all_to_all | solution.py:358
  27.2 0.0 all-reduce.3.cloned.1.call-start
  27.2 0.0 copy-done.4
  27.2 0.1 copy.22
  27.4 0.2 reduce-window.4
  27.5 0.1 reduce
  27.6 0.5 slice.7
  28.2 0.2 convert_reduce_fusion
  28.4 0.2 select_reduce_fusion
  28.7 0.7 compare_select_fusion
  29.3 0.7 compare_and_fusion
  30.0 37.6 %all-to-all-done = bf16[1,128,8,384]{3,2,0,1:T(8,128)(2,1)S(1)} async-done(((bf16[1,128,8,384]{3,2,0,1:T(8,128)(2,1)}), bf16[1,128,8,384]{3,2,0,1:T(8,128)(2,1)S(1)}, u32[]{:S(2)}, u32[]{:S(2)}) %all-to-all-start) | async-done | bytes 786464 | tf_op jit(solution)/shard_map/all_to_all | solution.py:358
  67.6 1.9 gather_fusion
  69.5 0.0 copy-done
  69.5 0.0 copy-start.5
  69.5 1.5 convolution_convert_fusion
  71.0 0.0 all-reduce.3.cloned.1.call-update
  71.1 0.0 copy-done.5
  71.1 1.1 pad.4
  72.2 0.0 copy-start.6
  72.2 0.0 copy-start.7
  72.2 0.0 copy-start.2
  72.2 0.0 copy-start.3
  72.2 1.6 copy.24.wqkv_ref
  73.8 0.0 copy-done.6
  73.8 0.0 copy-done.7
  74.5 51.6 %all-reduce.3.cloned.1.call-done.feats_ref = bf16[512,768]{1,0:T(8,128)(2,1)} async-done(((bf16[512,768]{1,0:T(8,128)(2,1)}), bf16[512,768]{1,0:T(8,128)(2,1)}) %all-reduce.3.cloned.1.call-update) | async-done | bytes 786448 | tf_op jit(solution)/shard_map/psum | solution.py:361
  126.1 0.0 copy-done.2
  126.1 0.0 copy-done.3
  126.1 0.0 copy-start.1
  126.1 1.1 copy-done.1
  127.2 57.4 %shard_map.112 = (f32[512,192]{1,0:T(8,128)S(1)}, f32[1,768]{1,0:T(1,128)S(1)}, f32[1,1]{1,0:T(1,128)}) custom-call(bf16[512,768]{1,0:T(8,128)(2,1)S(1)} %copy-done.1, s32[16,128]{1,0:T(8,128)S(1)} %bitcast.16, f32[1,768]{1,0:T(1,128)S(1)} %reshape.158.gain_ref, bf16[768,768]{1,0:T(8,128)(2,1)S(1)} %copy.24.wqkv_ref, bf16[192,768]{1,0:T(8,128)(2,1)S(1)} %copy-done.3, ...), custom_call_target="tpu_custom_call" | custom-call | tf_op jit(solution)/shard_map/pallas_call | solution.py:292
  184.6 0.9 copy.25
  185.5 0.6 copy.30
  (7 shorter events, 0.0 us)
Async XLA Ops:
  7.2 62.3 %copy-start = (bf16[384,768]{1,0:T(8,128)(2,1)S(1)}, bf16[384,768]{1,0:T(8,128)(2,1)}, u32[]{:S(2)}) copy-start(bf16[384,768]{1,0:T(8,128)(2,1)} %param.11) | copy-start | bytes 1769476
  7.2 20.0 %copy-start.4 = (s32[1,16,128]{2,1,0:T(8,128)S(1)}, s32[1,16,128]{2,1,0:T(8,128)}, u32[]{:S(2)}) copy-start(s32[1,16,128]{2,1,0:T(8,128)} %param.10) | copy-start | bytes 24580
  7.2 60.4 %all-to-all-start = ((bf16[1,128,8,384]{3,2,0,1:T(8,128)(2,1)}), bf16[1,128,8,384]{3,2,0,1:T(8,128)(2,1)S(1)}, u32[]{:S(2)}, u32[]{:S(2)}) async-start(bf16[1,128,8,384]{3,2,0,1:T(8,128)(2,1)} %bitcast.19), calls=%async_computation | async-start | bytes 1572864 | tf_op jit(solution)/shard_map/all_to_all | solution.py:358
  27.2 98.9 %all-reduce.3.cloned.1.call-start = ((), (), s32[]{:S(2)}) async-start(), calls=%async_computation.1 | async-start | bytes 1572864 | tf_op jit(solution)/shard_map/psum | solution.py:361
  69.5 1.6 copy-start.5
  72.2 1.7 copy-start.6
  72.2 1.7 copy-start.7
  72.2 53.9 %copy-start.2 = (bf16[256,768]{1,0:T(8,128)(2,1)S(1)}, bf16[256,768]{1,0:T(8,128)(2,1)}, u32[]{:S(2)}) copy-start(bf16[256,768]{1,0:T(8,128)(2,1)} %reports_ref.1) | copy-start | bytes 1179652
  72.2 53.9 %copy-start.3 = (bf16[192,768]{1,0:T(8,128)(2,1)S(1)}, bf16[192,768]{1,0:T(8,128)(2,1)}, u32[]{:S(2)}) copy-start(bf16[192,768]{1,0:T(8,128)(2,1)} %wout_ref.1) | copy-start | bytes 884740
  126.1 1.1 copy-start.1
Sparse Core Ops, SparseCore 0:
  71.2 54.8 all-reduce.2
